TPU v7x, 32 devices: a whole 2x2x4 slice. The times are simulated.
32 devices in a mesh: space: 8 (over z, x), feat: 4 (over y, core).
Axes of the slice: x: 2, y: 2, z: 4, core: 2. Of those that a mesh axis runs over, the one named last changes fastest.
Arguments:
- bond_state: bfloat16 [16384, 512], P('space', 'feat'), may hold values from -6 to 6
- block_fill: int32 [128], P('space'), may hold values from 64 to 128
- w_in: bfloat16 [512, 512], P(None, 'feat'), may hold values from -0.25 to 0.25
- w_down: bfloat16 [512, 64], P('feat'), may hold values from -0.25 to 0.25
- pair_coef: bfloat16 [896, 128, 128], P('space'), may hold values from -0.5 to 0.5
- pair_source: int32 [896], P('space'), may hold values from 0 to 15
- pair_owner: int32 [896, 1], P('space'), may hold values from 0 to 7; in each aligned block of 112 rows (0 to 111, 112 to 223, ...) at most 16 rows name the same one
- pair_target: int32 [896], P('space'), may hold values from 0 to 15
- w_gate: bfloat16 [64, 512], P(None, 'feat'), may hold values from -0.75 to 0.75
- w_atom_in: bfloat16 [64, 256], P(None, 'feat'), may hold values from -0.75 to 0.75
- atom_state: bfloat16 [256, 4096], P('feat', 'space'), may hold values from -6 to 6
- w_atom: bfloat16 [256, 256], P('feat'), may hold values from -0.375 to 0.375
- bond_ends: int32 [2, 16384], P(None, 'space'), may hold values from 0 to 1535
- w_left: bfloat16 [256, 512], P(None, 'feat'), may hold values from -0.375 to 0.375
- w_right: bfloat16 [256, 512], P(None, 'feat'), may hold values from -0.375 to 0.375
Outputs:
- bond_out: bfloat16 [16384, 512], P('space', 'feat')
- atom_out: bfloat16 [256, 4096], P('feat', 'space')
Inputs may be any that keep to these rules, and one draw needn't show every extreme that they name: `pair_owner`: among the 112 pairs of one domain, at most 16 name the same owner, a bound that some block reaches.
All inputs are finite; a program needn't handle non-finite values.
Results may differ from a plain program's by a relative error of at most 0.008.
Values may be sent and summed in bfloat16 or wider, within the bound.
A program may use at most 64 MiB of HBM per device.

v0:
```python
import jax
import jax.numpy as jnp
from jax import lax
from jax.sharding import PartitionSpec as P


def passed_along(value, axis, steps):
    count = lax.axis_size(axis)
    pairs = [(source, (source + steps) % count) for source in range(count)]
    return lax.ppermute(value, axis, pairs)


def extended(cells, sides, width):
    for axis, dim in sides:
        count = lax.axis_size(axis)
        head = lax.slice_in_dim(cells, 0, width, axis=dim)
        tail = lax.slice_in_dim(cells, cells.shape[dim] - width, cells.shape[dim], axis=dim)
        cells = jnp.concatenate(
            [
                lax.ppermute(tail, axis, [(i, (i + 1) % count) for i in range(count)]),
                cells,
                lax.ppermute(head, axis, [((i + 1) % count, i) for i in range(count)]),
            ],
            axis=dim,
        )
    return cells


def local(
    bond_state,
    block_fill,
    w_in,
    w_down,
    pair_coef,
    pair_source,
    pair_owner,
    pair_target,
    w_gate,
    w_atom_in,
    atom_state,
    w_atom,
    bond_ends,
    w_left,
    w_right,
):
    bond_slots = bond_state.shape[0]
    blocks = block_fill.shape[0]
    block_size = bond_slots // blocks
    pair_count = pair_source.shape[0]
    spaces = lax.axis_size("space")
    feat_count = lax.axis_size("feat")
    capacity = max(2, min(blocks, 2 * pair_count // spaces))
    channels = w_down.shape[1]
    own_channels = channels // feat_count
    atom_cols = atom_state.shape[1]
    contract_first = (((0,), (0,)), ((), ()))
    position = lax.broadcasted_iota(jnp.int32, (blocks, block_size), 1)
    real_mask = (position < block_fill[:, None]).astype(jnp.float32).reshape(bond_slots)
    full_rows = lax.all_gather(bond_state, "feat", axis=1, tiled=True)
    whole_in, whole_down = (
        lax.all_gather(w_in, "feat", axis=1, tiled=True),
        lax.all_gather(w_down, "feat", axis=0, tiled=True),
    )
    all_hidden = jax.nn.silu(
        jnp.dot(full_rows, whole_in, preferred_element_type=jnp.float32)
    ).astype(jnp.bfloat16)
    own_units = w_in.shape[1]
    hidden = lax.dynamic_slice_in_dim(all_hidden, lax.axis_index("feat") * own_units, own_units, 1)
    down_columns = lax.dynamic_slice_in_dim(
        whole_down, lax.axis_index("feat") * own_channels, own_channels, 1
    )
    angular_sum = lax.dot_general(
        down_columns, all_hidden, (((0,), (1,)), ((), ())), preferred_element_type=jnp.float32
    )
    angular = (angular_sum * real_mask[None, :]).astype(jnp.bfloat16)
    angular_blocks = angular.reshape(own_channels, blocks, block_size)
    sources = jnp.take(angular_blocks, pair_source, axis=1)
    contrib = jnp.einsum(
        "cpj,pij->pci", sources, pair_coef, preferred_element_type=jnp.float32
    ).astype(jnp.bfloat16)
    owner_ids = pair_owner[:, 0]
    owner_table = (
        owner_ids[:, None] == lax.broadcasted_iota(jnp.int32, (pair_count, spaces), 1)
    ).astype(jnp.int32)
    slot_rank = jnp.sum(jnp.cumsum(owner_table, axis=0) * owner_table, axis=1) - 1
    flat_slot = owner_ids * capacity + slot_rank
    outgoing = (
        jnp.zeros((spaces * capacity, own_channels, block_size), jnp.bfloat16)
        .at[flat_slot]
        .set(contrib)
    )
    labels = jnp.full((spaces * capacity,), blocks, jnp.int32).at[flat_slot].set(pair_target)
    incoming, arrived = (
        lax.all_to_all(
            outgoing.reshape(spaces, capacity, own_channels, block_size),
            "space",
            split_axis=0,
            concat_axis=0,
            tiled=True,
        ),
        lax.all_to_all(
            labels.reshape(spaces, capacity), "space", split_axis=0, concat_axis=0, tiled=True
        ),
    )
    chooser = (
        arrived.reshape(spaces * capacity)[None, :]
        == lax.broadcasted_iota(jnp.int32, (blocks, spaces * capacity), 0)
    ).astype(jnp.bfloat16)
    block_sums = jnp.einsum(
        "kq,qcr->ckr",
        chooser,
        incoming.reshape(spaces * capacity, own_channels, block_size),
        preferred_element_type=jnp.float32,
    )
    message = (block_sums.reshape(own_channels, bond_slots) * real_mask[None, :]).astype(
        jnp.bfloat16
    )
    shard_piece = lax.all_gather(message, "feat", axis=0, tiled=True)
    gate_pre = lax.dot_general(
        shard_piece, w_gate, contract_first, preferred_element_type=jnp.float32
    )
    to_atoms = lax.dot_general(
        shard_piece, w_atom_in, contract_first, preferred_element_type=jnp.float32
    )
    window = 3 * atom_cols
    window_sums = jax.ops.segment_sum(to_atoms, bond_ends[1], num_segments=window).T
    window_counts = jax.ops.segment_sum(real_mask, bond_ends[1], num_segments=window)
    from_upper = (
        passed_along(window_sums[:, :atom_cols].astype(jnp.bfloat16), "space", -1).astype(
            jnp.float32
        ),
        passed_along(window_counts[:atom_cols].astype(jnp.bfloat16), "space", -1).astype(
            jnp.float32
        ),
    )
    from_lower = (
        passed_along(window_sums[:, 2 * atom_cols :].astype(jnp.bfloat16), "space", 1).astype(
            jnp.float32
        ),
        passed_along(window_counts[2 * atom_cols :].astype(jnp.bfloat16), "space", 1).astype(
            jnp.float32
        ),
    )
    atom_sums = window_sums[:, atom_cols : 2 * atom_cols] + from_upper[0] + from_lower[0]
    atom_counts = window_counts[atom_cols : 2 * atom_cols] + from_upper[1] + from_lower[1]
    mean_in = (atom_sums / jnp.maximum(atom_counts, 1.0)[None, :]).astype(jnp.bfloat16)
    partial_pre = lax.dot_general(
        w_atom, mean_in, contract_first, preferred_element_type=jnp.float32
    )
    own_pre = lax.psum_scatter(
        partial_pre.astype(jnp.bfloat16), "feat", scatter_dimension=0, tiled=True
    ).astype(jnp.float32)
    atom_out = (atom_state + jax.nn.silu(own_pre)).astype(jnp.bfloat16)
    own_window = extended(atom_out, (("space", 1),), atom_cols)
    neighbours = lax.all_gather(own_window, "feat", axis=0, tiled=True)
    left_rows = jnp.take(neighbours, bond_ends[0], axis=1)
    right_rows = jnp.take(neighbours, bond_ends[1], axis=1)
    mixed_atoms = lax.dot_general(
        left_rows, w_left, contract_first, preferred_element_type=jnp.float32
    ) + lax.dot_general(right_rows, w_right, contract_first, preferred_element_type=jnp.float32)
    update = jax.nn.sigmoid(gate_pre) * (hidden.astype(jnp.float32) + jax.nn.silu(mixed_atoms))
    bond_out = (bond_state + real_mask[:, None] * update).astype(jnp.bfloat16)
    return (bond_out, atom_out)


def solution(mesh):
    placed = (
        P("space", "feat"),
        P("space"),
        P(None, "feat"),
        P("feat", None),
        P("space", None, None),
        P("space"),
        P("space", None),
        P("space"),
        P(None, "feat"),
        P(None, "feat"),
        P("feat", "space"),
        P("feat", None),
        P(None, "space"),
        P(None, "feat"),
        P(None, "feat"),
    )
    return jax.shard_map(
        local,
        mesh=mesh,
        in_specs=placed,
        out_specs=(P("space", "feat"), P("feat", "space")),
        check_vma=False,
    )
```

profile of v0, /device:TPU:0, one launch (start us, length us, event | category | flops | bytes accessed | tf_op | source)
XLA Modules:
  0.0 172.4 jit_solution(8166564633234822247)
XLA Ops:
  7.2 0.7 all-gather.2.cloned.1.call-update
  7.9 0.7 fusion.36
  8.8 0.8 select_reduce_fusion
  9.7 0.7 fusion.48
  10.3 1.1 scatter_custom_fusion.1
  11.4 0.7 all_to_all.10
  12.1 7.3 %all-to-all-start.1 = ((s32[8,1,16]{2,1,0:T(1,128)}), s32[8,1,16]{2,1,0:T(1,128)S(1)}, u32[]{:S(2)}, u32[]{:S(2)}) async-start(s32[8,1,16]{2,1,0:T(1,128)} %bitcast.7), calls=%async_computation.1 | async-start | bytes 8192 | tf_op jit(solution)/shard_map/all_to_all | solution.py:101
  19.3 5.9 %all_gather.15 = bf16[512,64]{0,1:T(8,128)(2,1)S(1)} all-gather(bf16[128,64]{0,1:T(8,128)(2,1)} %param.20), channel_id=1, replica_groups=mesh['space'=8,'feat'=4] {'feat'}, dimensions={0}, use_global_device_ids=true | all-gather | bytes 81920 | tf_op jit(solution)/shard_map/all_gather | solution.py:62
  25.2 0.7 compare_select_fusion.2
  25.9 10.8 %all_gather.17 = bf16[512,512]{1,0:T(8,128)(2,1)S(1)} all-gather(bf16[512,128]{1,0:T(8,128)(2,1)} %param.19), channel_id=1, replica_groups=mesh['space'=8,'feat'=4] {'feat'}, dimensions={1}, use_global_device_ids=true | all-gather | bytes 655360 | tf_op jit(solution)/shard_map/all_gather | solution.py:61
  36.7 0.7 compare_and_fusion.2
  37.3 0.7 convert_bitcast_fusion
  38.1 0.2 all-gather.2.cloned.1.call-done
  38.3 3.4 %multiply_convert_fusion = bf16[2048,512]{1,0:T(8,128)(2,1)S(1)} fusion(bf16[2048,512]{1,0:T(8,128)(2,1)} %all-gather.2.cloned.1.call-done, bf16[512,512]{1,0:T(8,128)(2,1)S(1)} %all_gather.17), kind=kOutput, calls=%fused_computation.7 | convolution fusion | flops 1078984704 | bytes 4718592 | tf_op jit(solution)/shard_map/dot_general | solution.py:65
  41.7 1.3 copy-done.1
  43.0 0.6 fusion.9
  43.7 0.7 gather_fusion
  44.4 4.1 %convolution_convert_fusion = bf16[112,16,128]{2,1,0:T(8,128)(2,1)S(1)} fusion(bf16[112,128,128]{2,1,0:T(8,128)(2,1)} %param.21, bf16[112,16,128]{2,1,0:T(8,128)(2,1)S(1)} %gather_fusion, pred[112]{0:T(512)(128)(4,1)S(1)} %compare_and_fusion.2), kind=kOutput, calls=%fused_computation.19 | convolution fusion | flops 59179008 | bytes 4587632 | tf_op jit(solution)/shard_map/cpj,pij->pci/dot_general | solution.py:78
  48.6 3.9 %scatter_fusion = bf16[128,16,128]{2,1,0:T(8,128)(2,1)S(1)} fusion(bf16[128,16,128]{2,1,0:T(8,128)(2,1)S(1)} %broadcast_in_dim.37, s32[112]{0:T(128)S(1)} %fusion.48, bf16[112,16,128]{2,1,0:T(8,128)(2,1)S(1)} %convolution_convert_fusion), kind=kCustom, calls=%fused_computation.3 | custom fusion | bytes 1376704 | tf_op jit(solution)/shard_map/scatter | solution.py:90
  52.5 0.9 copy.25
  53.5 5.9 %all-to-all-start = ((bf16[8,16,16,128]{3,1,2,0:T(8,128)(2,1)}), bf16[8,16,16,128]{3,1,2,0:T(8,128)(2,1)S(1)}, u32[]{:S(2)}, u32[]{:S(2)}) async-start(bf16[8,16,16,128]{3,1,2,0:T(8,128)(2,1)} %copy.25), calls=%async_computation | async-start | bytes 1048576 | tf_op jit(solution)/shard_map/all_to_all | solution.py:94
  59.4 13.2 %scatter_custom_fusion.3 = f32[1536]{0:T(1024)S(1)} fusion(s32[2048]{0:T(1024)S(1)} %bitcast.59, f32[2048]{0:T(1024)S(1)} %convert_bitcast_fusion, f32[]{:T(128)} %constant.38.clone.1), kind=kCustom, calls=%fused_computation.70 | custom fusion | flops 2048 | bytes 6148 | tf_op jit(solution)/shard_map/scatter-add | solution.py:127
  72.7 4.8 %collective-permute-start.2 = (bf16[512]{0:T(512)(128)(2,1)S(1)}, bf16[512]{0:T(512)(128)(2,1)S(1)}, u32[]{:S(2)}, u32[]{:S(2)}) collective-permute-start(bf16[512]{0:T(512)(128)(2,1)S(1)} %get-tuple-element.13), channel_id=1, source_target_pairs={{0,28},{4,0},{8,4},{12,8},{16,12},{20,16},{24,20},{28,24},{1,29},{... | collective-permute-start | bytes 3080 | tf_op jit(solution)/shard_map/ppermute | solution.py:10
  77.4 0.5 broadcast.123
  78.0 0.7 reduce.3
  78.8 0.2 fusion.39
  79.0 5.8 %all_gather.18 = bf16[64,2048]{1,0:T(8,128)(2,1)S(1)} all-gather(bf16[16,2048]{1,0:T(8,128)(2,1)S(1)} %fusion.34), channel_id=1, replica_groups=mesh['space'=8,'feat'=4] {'feat'}, dimensions={0}, use_global_device_ids=true | all-gather | bytes 327680 | tf_op jit(solution)/shard_map/all_gather | solution.py:118
  84.8 0.3 fusion.58
  85.1 11.7 %scatter_custom_fusion.2 = f32[1536,64]{1,0:T(8,128)S(1)} fusion(s32[2048]{0:T(1024)S(1)} %bitcast.60, f32[2048,64]{1,0:T(8,128)S(1)} %fusion.58, f32[]{:T(128)} %constant.38.clone.1), kind=kCustom, calls=%fused_computation.36 | custom fusion | flops 131072 | bytes 393220 | tf_op jit(solution)/shard_map/scatter-add | solution.py:126
  96.9 4.8 %collective-permute-start = (bf16[64,512]{0,1:T(8,128)(2,1)S(1)}, bf16[64,512]{0,1:T(8,128)(2,1)S(1)}, u32[]{:S(2)}, u32[]{:S(2)}) collective-permute-start(bf16[64,512]{0,1:T(8,128)(2,1)S(1)} %get-tuple-element.9), channel_id=1, source_target_pairs={{0,28},{4,0},{8,4},{12,8},{16,12},{20,16},{24,20},{28,24},{1,29},{... | collective-permute-start | bytes 196616 | tf_op jit(solution)/shard_map/ppermute | solution.py:10
  101.7 3.2 %collective-permute-done = bf16[64,512]{0,1:T(8,128)(2,1)S(1)} collective-permute-done((bf16[64,512]{0,1:T(8,128)(2,1)S(1)}, bf16[64,512]{0,1:T(8,128)(2,1)S(1)}, u32[]{:S(2)}, u32[]{:S(2)}) %collective-permute-start) | collective-permute-done | bytes 65568 | tf_op jit(solution)/shard_map/ppermute | solution.py:10
  104.9 4.9 %collective-permute-done.1 = bf16[64,512]{0,1:T(8,128)(2,1)S(1)} collective-permute-done((bf16[64,512]{0,1:T(8,128)(2,1)S(1)}, bf16[64,512]{0,1:T(8,128)(2,1)S(1)}, u32[]{:S(2)}, u32[]{:S(2)}) %collective-permute-start.1) | collective-permute-done | bytes 65568 | tf_op jit(solution)/shard_map/ppermute | solution.py:10
  109.8 0.3 fusion.8
  110.1 0.9 copy.35
  111.2 16.6 %reduce-scatter.4.cloned.1.call-done = bf16[64,512]{1,0:T(8,128)(2,1)} async-done(((bf16[256,512]{1,0:T(8,128)(2,1)}), bf16[64,512]{1,0:T(8,128)(2,1)}) %reduce-scatter.4.cloned.1.call-update) | async-done | bytes 65552
  127.7 1.0 copy.36
  128.8 1.5 collective-permute-start.4
  130.3 3.3 %collective-permute-start.5 = (bf16[64,512]{0,1:T(8,128)(2,1)S(1)}, bf16[64,512]{0,1:T(8,128)(2,1)S(1)}, u32[]{:S(2)}, u32[]{:S(2)}) collective-permute-start(bf16[64,512]{0,1:T(8,128)(2,1)S(1)} %fusion.31), channel_id=1, source_target_pairs={{4,0},{8,4},{12,8},{16,12},{20,16},{24,20},{28,24},{0,28},{5,1},{9... | collective-permute-start | bytes 196616 | tf_op jit(solution)/shard_map/ppermute | solution.py:22
  133.6 0.7 copy.33
  134.3 2.3 %collective-permute-done.4 = bf16[64,512]{0,1:T(8,128)(2,1)S(1)} collective-permute-done((bf16[64,512]{0,1:T(8,128)(2,1)S(1)}, bf16[64,512]{0,1:T(8,128)(2,1)S(1)}, u32[]{:S(2)}, u32[]{:S(2)}) %collective-permute-start.4) | collective-permute-done | bytes 65568 | tf_op jit(solution)/shard_map/ppermute | solution.py:20
  136.6 1.3 collective-permute-done.5
  138.2 7.8 %all_gather.19 = bf16[256,1536]{1,0:T(8,128)(2,1)S(1)} all-gather(bf16[64,1536]{1,0:T(8,128)(2,1)S(1)} %copy.30), channel_id=1, replica_groups=mesh['space'=8,'feat'=4] {'feat'}, dimensions={0}, use_global_device_ids=true | all-gather | bytes 983040 | tf_op jit(solution)/shard_map/all_gather | solution.py:155
  146.0 0.3 copy.31
  146.3 7.5 %gather_fusion.1 = bf16[2048,256]{1,0:T(8,128)(2,1)S(1)} fusion(bf16[256,1536]{0,1:T(8,128)(2,1)S(1)} %copy.31, s32[2048]{0:T(1024)S(1)} %fusion.41), kind=kCustom, calls=%fused_computation.clone | custom fusion | bytes 2105344 | tf_op jit(solution)/shard_map/jit(_take)/gather | solution.py:156
  153.8 7.5 %gather_fusion.2 = bf16[2048,256]{1,0:T(8,128)(2,1)S(1)} fusion(bf16[256,1536]{0,1:T(8,128)(2,1)S(1)} %copy.31, s32[2048]{0:T(1024)S(1)} %fusion.42), kind=kCustom, calls=%fused_computation.1.clone | custom fusion | bytes 2105344 | tf_op jit(solution)/shard_map/jit(_take)/gather | solution.py:157
  161.4 0.8 fusion.11
  162.1 0.8 convolution_add_fusion
  162.9 2.6 %fusion.6 = bf16[2048,128]{1,0:T(8,128)(2,1)} fusion(bf16[64,2048]{1,0:T(8,128)(2,1)S(1)} %all_gather.18, bf16[64,128]{1,0:T(8,128)(2,1)S(1)} %copy-done.8, f32[2048,128]{1,0:T(8,128)S(1)} %convolution_add_fusion, bf16[2048,128]{1,0:T(8,128)(2,1)S(1)} %copy-done.2, bf16[2048,512]{1,0:T(8,128)(2,1)} %copy-done.1, s32[]{:T(128)S(6)} %select_n.31, ...), kind=kOutput, calls=%fused_computation.16 | convolution fusion | flops 37224448 | bytes 2908164 | tf_op jit(solution)/shard_map/dot_general | solution.py:119
  (47 shorter events, 1.2 us)
Async XLA Ops:
  7.2 154.2 %copy-start = (bf16[256,128]{1,0:T(8,128)(2,1)S(1)}, bf16[256,128]{1,0:T(8,128)(2,1)}, u32[]{:S(2)}) copy-start(bf16[256,128]{1,0:T(8,128)(2,1)} %param.30) | copy-start | bytes 196612
  7.2 31.1 %all-gather.2.cloned.1.call-start = ((), (), s32[]{:S(2)}) async-start(), calls=%async_computation.3 | async-start | bytes 2621440 | tf_op jit(solution)/shard_map/all_gather | solution.py:59
  12.1 41.4 %all-to-all-start.1 = ((s32[8,1,16]{2,1,0:T(1,128)}), s32[8,1,16]{2,1,0:T(1,128)S(1)}, u32[]{:S(2)}, u32[]{:S(2)}) async-start(s32[8,1,16]{2,1,0:T(1,128)} %bitcast.7), calls=%async_computation.1 | async-start | bytes 8192 | tf_op jit(solution)/shard_map/all_to_all | solution.py:101
  41.7 1.4 copy-start.1
  44.4 15.0 %copy-start.5 = (s32[2,2048]{1,0:T(2,128)S(1)}, s32[2,2048]{1,0:T(2,128)}, u32[]{:S(2)}) copy-start(s32[2,2048]{1,0:T(2,128)} %param.29) | copy-start | bytes 49156
  48.5 36.3 %copy-start.6 = (bf16[64,64]{1,0:T(8,128)(2,1)S(1)}, bf16[64,64]{1,0:T(8,128)(2,1)}, u32[]{:S(2)}) copy-start(bf16[64,64]{1,0:T(8,128)(2,1)} %param.26) | copy-start | bytes 24580
  53.5 56.4 %copy-start.7 = (bf16[64,256]{1,0:T(8,128)(2,1)S(1)}, bf16[64,256]{1,0:T(8,128)(2,1)}, u32[]{:S(2)}) copy-start(bf16[64,256]{1,0:T(8,128)(2,1)} %param.28) | copy-start | bytes 98308
  53.5 25.2 %all-to-all-start = ((bf16[8,16,16,128]{3,1,2,0:T(8,128)(2,1)}), bf16[8,16,16,128]{3,1,2,0:T(8,128)(2,1)S(1)}, u32[]{:S(2)}, u32[]{:S(2)}) async-start(bf16[8,16,16,128]{3,1,2,0:T(8,128)(2,1)} %copy.25), calls=%async_computation | async-start | bytes 1048576 | tf_op jit(solution)/shard_map/all_to_all | solution.py:94
  59.3 68.4 %reduce-scatter.4.cloned.1.call-start = ((), (), s32[]{:S(2)}) async-start(), calls=%async_computation.4 | async-start | bytes 327680
  72.7 29.0 %collective-permute-start.2 = (bf16[512]{0:T(512)(128)(2,1)S(1)}, bf16[512]{0:T(512)(128)(2,1)S(1)}, u32[]{:S(2)}, u32[]{:S(2)}) collective-permute-start(bf16[512]{0:T(512)(128)(2,1)S(1)} %get-tuple-element.13), channel_id=1, source_target_pairs={{0,28},{4,0},{8,4},{12,8},{16,12},{20,16},{24,20},{28,24},{1,29},{... | collective-permute-start | bytes 3080 | tf_op jit(solution)/shard_map/ppermute | solution.py:10
  77.4 24.2 %collective-permute-start.3 = (bf16[512]{0:T(512)(128)(2,1)S(1)}, bf16[512]{0:T(512)(128)(2,1)S(1)}, u32[]{:S(2)}, u32[]{:S(2)}) collective-permute-start(bf16[512]{0:T(512)(128)(2,1)S(1)} %get-tuple-element.14), channel_id=1, source_target_pairs={{0,4},{4,8},{8,12},{12,16},{16,20},{20,24},{24,28},{28,0},{1,5},{5... | collective-permute-start | bytes 3080 | tf_op jit(solution)/shard_map/ppermute | solution.py:10
  78.8 32.2 %copy-start.3 = (bf16[64,512]{1,0:T(8,128)(2,1)S(1)}, bf16[64,512]{1,0:T(8,128)(2,1)}, u32[]{:S(2)}) copy-start(bf16[64,512]{1,0:T(8,128)(2,1)} %param.27) | copy-start | bytes 196612
  96.9 8.0 %collective-permute-start = (bf16[64,512]{0,1:T(8,128)(2,1)S(1)}, bf16[64,512]{0,1:T(8,128)(2,1)S(1)}, u32[]{:S(2)}, u32[]{:S(2)}) collective-permute-start(bf16[64,512]{0,1:T(8,128)(2,1)S(1)} %get-tuple-element.9), channel_id=1, source_target_pairs={{0,28},{4,0},{8,4},{12,8},{16,12},{20,16},{24,20},{28,24},{1,29},{... | collective-permute-start | bytes 196616 | tf_op jit(solution)/shard_map/ppermute | solution.py:10
  101.6 8.2 %collective-permute-start.1 = (bf16[64,512]{0,1:T(8,128)(2,1)S(1)}, bf16[64,512]{0,1:T(8,128)(2,1)S(1)}, u32[]{:S(2)}, u32[]{:S(2)}) collective-permute-start(bf16[64,512]{0,1:T(8,128)(2,1)S(1)} %get-tuple-element.10), channel_id=1, source_target_pairs={{0,4},{4,8},{8,12},{12,16},{16,20},{20,24},{24,28},{28,0},{1,5},{5... | collective-permute-start | bytes 196616 | tf_op jit(solution)/shard_map/ppermute | solution.py:10
  128.8 7.8 %collective-permute-start.4 = (bf16[64,512]{0,1:T(8,128)(2,1)S(1)}, bf16[64,512]{0,1:T(8,128)(2,1)S(1)}, u32[]{:S(2)}, u32[]{:S(2)}) collective-permute-start(bf16[64,512]{0,1:T(8,128)(2,1)S(1)} %fusion.31), channel_id=1, source_target_pairs={{0,4},{4,8},{8,12},{12,16},{16,20},{20,24},{24,28},{28,0},{1,5},{5... | collective-permute-start | bytes 196616 | tf_op jit(solution)/shard_map/ppermute | solution.py:20
  130.3 7.6 %collective-permute-start.5 = (bf16[64,512]{0,1:T(8,128)(2,1)S(1)}, bf16[64,512]{0,1:T(8,128)(2,1)S(1)}, u32[]{:S(2)}, u32[]{:S(2)}) collective-permute-start(bf16[64,512]{0,1:T(8,128)(2,1)S(1)} %fusion.31), channel_id=1, source_target_pairs={{4,0},{8,4},{12,8},{16,12},{20,16},{24,20},{28,24},{0,28},{5,1},{9... | collective-permute-start | bytes 196616 | tf_op jit(solution)/shard_map/ppermute | solution.py:22
  153.8 8.3 %copy-start.4 = (bf16[256,128]{1,0:T(8,128)(2,1)S(1)}, bf16[256,128]{1,0:T(8,128)(2,1)}, u32[]{:S(2)}) copy-start(bf16[256,128]{1,0:T(8,128)(2,1)} %param.31) | copy-start | bytes 196612
  161.3 1.6 copy-start.2
  161.4 1.6 copy-start.8
Sparse Core Ops, SparseCore 0:
  9.5 28.6 all-gather.1
  111.1 16.5 reduce-scatter.3
where the time goes:
time: 173 us; the launch traced here: 172 us
  other arithmetic  30.3 us (18%)
  blocking collectives  30.3 us (18%)
  waiting for transfers between devices  29.3 us (17%)
  starting transfers between devices  27.6 us (16%)
  local copies, waits for them, and re-layouts  27.5 us (16%)
  between operations  14.4 us (8%)
  matrix products  13.1 us (8%)
    unnamed x3, waiting for transfers between devices  17.3 us
    scatter-add x1, other arithmetic, local(): jax.ops.segment_sum(real_mask, bond_ends[1], num_segments=window)  13.2 us
    scatter-add x1, other arithmetic, local(): jax.ops.segment_sum(to_atoms, bond_ends[1], num_segments=window)  11.7 us
    all_gather x1, blocking collectives, local(): lax.all_gather(w_in, 'feat', axis=1, tiled=True)  10.8 us
    ppermute x4, starting transfers between devices, passed_along(): return lax.ppermute(value, axis, pairs)  9.55 us
    ppermute x4, waiting for transfers between devices, passed_along(): return lax.ppermute(value, axis, pairs)  8.14 us
    all_gather x1, blocking collectives, local(): neighbours = lax.all_gather(own_window, 'feat', axis=0, tiled=True)  7.84 us
    gather x1, local copies, waits for them, and re-layouts, local(): left_rows = jnp.take(neighbours, bond_ends[0], axis=1)  7.5 us
  transfers between devices with their start and end apart: 10, of which 6 were waited for; matrix products, arithmetic and copies ran while one was open for 27% of the time, Pallas kernels for 0%

commit v1 on v0

--- a/solution.py
+++ b/solution.py
@@ -1,6 +1,10 @@
+import functools
+
 import jax
 import jax.numpy as jnp
 from jax import lax
+from jax.experimental import pallas as pl
+from jax.experimental.pallas import tpu as pltpu
 from jax.sharding import PartitionSpec as P
 
 
@@ -163,6 +167,473 @@
     return (bond_out, atom_out)
 
 
+MESH_IDS = pl.DeviceIdType.MESH
+
+
+def silu(value):
+    return value / (1.0 + jnp.exp(-value))
+
+
+def greet(peers):
+    barrier = pltpu.get_barrier_semaphore()
+    for peer in peers:
+        pl.semaphore_signal(barrier, inc=1, device_id=peer, device_id_type=MESH_IDS)
+    pl.semaphore_wait(barrier, len(peers))
+
+
+def remote(source, target, sends, receives, number, peer):
+    return pltpu.make_async_remote_copy(
+        src_ref=source,
+        dst_ref=target,
+        send_sem=sends.at[number],
+        recv_sem=receives.at[number],
+        device_id=peer,
+        device_id_type=MESH_IDS,
+    )
+
+
+def feat_peers(count):
+    space, feat = lax.axis_index("space"), lax.axis_index("feat")
+    return [(space, lax.rem(feat + step, count)) for step in range(1, count)]
+
+
+def down(value, step):
+    count = lax.axis_size("space")
+    return lax.rem(value + step + count, count)
+
+
+def bond_kernel(
+    feats,
+    fill,
+    bond,
+    w_in,
+    w_down,
+    state,
+    angular,
+    hidden,
+    state_window,
+    rows,
+    whole_in,
+    whole_down,
+    angular_rows,
+    sends,
+    receives,
+):
+    space, feat = lax.axis_index("space"), lax.axis_index("feat")
+    share = bond.shape[0] // feats
+    width, units = bond.shape[1], w_in.shape[1]
+    own_channels = angular.shape[0]
+    atoms = state.shape[1]
+    block_size = bond.shape[0] // fill.shape[0]
+    peers = feat_peers(feats)
+    lower, upper = (down(space, -1), feat), (down(space, 1), feat)
+    greet(peers + [lower, upper])
+    own_width = pl.ds(pl.multiple_of(feat * width, width), width)
+    own_units = pl.ds(pl.multiple_of(feat * units, units), units)
+    copies, late = [], []
+    number = 0
+    for peer in peers:
+        their_rows = pl.ds(pl.multiple_of(peer[1] * share, share), share)
+        copies.append(remote(w_in, whole_in.at[:, own_units], sends, receives, number, peer))
+        copies.append(
+            remote(bond.at[their_rows], rows.at[:, own_width], sends, receives, number + 1, peer)
+        )
+        copies.append(remote(w_down, whole_down.at[own_units], sends, receives, number + 2, peer))
+        number += 3
+    late.append(
+        remote(state, state_window.at[:, 2 * atoms :], sends, receives, number, lower)
+    )
+    late.append(
+        remote(state, state_window.at[:, :atoms], sends, receives, number + 1, upper)
+    )
+    number += 2
+    for copy in copies + late:
+        copy.start()
+    own_rows = pl.ds(pl.multiple_of(feat * share, share), share)
+    rows[:, own_width] = bond[own_rows]
+    whole_in[:, own_units] = w_in[...]
+    whole_down[own_units] = w_down[...]
+    state_window[:, atoms : 2 * atoms] = state[...]
+    for copy in copies:
+        copy.wait()
+    hidden[...] = silu(
+        jnp.dot(rows[...], whole_in[...], preferred_element_type=jnp.float32)
+    ).astype(jnp.bfloat16)
+    sums = lax.dot_general(
+        whole_down[...], hidden[...], (((0,), (1,)), ((), ())), preferred_element_type=jnp.float32
+    )
+    for part in range(share // block_size):
+        limit = fill[feat * (share // block_size) + part]
+        place = lax.broadcasted_iota(jnp.int32, (1, block_size), 1)
+        mask = jnp.where(place < limit, 1.0, 0.0)
+        span = slice(part * block_size, (part + 1) * block_size)
+        angular_rows[:, span] = (sums[:, span] * mask).astype(jnp.bfloat16)
+    own_span = pl.ds(pl.multiple_of(feat * share, share), share)
+    back = []
+    for peer in peers:
+        theirs = pl.ds(pl.multiple_of(peer[1] * own_channels, own_channels), own_channels)
+        back.append(
+            remote(
+                angular_rows.at[theirs], angular.at[:, own_span], sends, receives, number, peer
+            )
+        )
+        number += 1
+    for copy in back:
+        copy.start()
+    mine = pl.ds(pl.multiple_of(feat * own_channels, own_channels), own_channels)
+    angular[:, own_span] = angular_rows[mine]
+    for copy in back + late:
+        copy.wait()
+
+
+def pair_kernel(steps, blocks, source, owner, target, angular, coefficients, outgoing, total):
+    step = pl.program_id(0)
+    count = coefficients.shape[0]
+    block_size = coefficients.shape[1]
+    group = 14 if count % 14 == 0 else 1
+
+    @pl.when(step == 0)
+    def clear():
+        total[...] = jnp.zeros_like(total)
+
+    def several(turn, carry):
+        products = []
+        for offset in range(group):
+            place = turn * group + offset
+            start = pl.multiple_of(source[step * count + place] * block_size, block_size)
+            products.append(
+                lax.dot_general(
+                    angular[:, pl.ds(start, block_size)],
+                    coefficients[place],
+                    (((1,), (1,)), ((), ())),
+                    preferred_element_type=jnp.float32,
+                )
+            )
+        for offset in range(group):
+            pair = step * count + turn * group + offset
+            slot = owner[pair] * blocks + target[pair]
+            total[slot] += products[offset]
+        return carry
+
+    lax.fori_loop(0, count // group, several, 0)
+
+    @pl.when(step == steps - 1)
+    def finish():
+        outgoing[...] = total[...].astype(jnp.bfloat16)
+
+
+def update_kernel(
+    spaces,
+    feats,
+    fill,
+    outgoing,
+    hidden_rows,
+    state_window,
+    bond,
+    ends,
+    w_gate,
+    w_atom_in,
+    w_atom,
+    w_left,
+    w_right,
+    bond_out,
+    atom_out,
+    incoming,
+    left_hot,
+    right_hot,
+    summed,
+    message,
+    halo_out,
+    halo_in,
+    mean,
+    means,
+    states,
+    whole_atom_in,
+    whole_atom,
+    hidden,
+    window_atoms,
+    space_sends,
+    space_receives,
+    sends,
+    receives,
+):
+    space, feat = lax.axis_index("space"), lax.axis_index("feat")
+    blocks = fill.shape[0]
+    slots = bond.shape[0]
+    size = slots // blocks
+    channels = summed.shape[0] // 2
+    width = bond.shape[1]
+    share = slots // feats
+    window = state_window.shape[1]
+    atoms = window // 3
+    inner = w_atom.shape[0]
+    peers = feat_peers(feats)
+    lower, upper = down(space, -1), down(space, 1)
+    sides = [(lower, feat), (upper, feat)]
+    diagonal = [(side, peer[1]) for side in (lower, upper) for peer in peers]
+    far = [(down(space, step), feat) for step in range(2, spaces - 1)]
+    greet(peers + sides + diagonal + far)
+    crossing = []
+    for step in range(1, spaces):
+        goal = down(space, step)
+        crossing.append(
+            remote(
+                outgoing.at[pl.ds(goal * blocks, blocks)],
+                incoming.at[space],
+                space_sends,
+                space_receives,
+                step,
+                (goal, feat),
+            )
+        )
+    for copy in crossing:
+        copy.start()
+    own_inner = pl.ds(pl.multiple_of(feat * inner, inner), inner)
+    own_span = pl.ds(pl.multiple_of(feat * share, share), share)
+    weights, returned = [], []
+    number = 0
+    for peer in peers:
+        theirs = pl.ds(pl.multiple_of(peer[1] * width, width), width)
+        weights.append(
+            remote(w_atom_in, whole_atom_in.at[feat], sends, receives, number, peer)
+        )
+        weights.append(remote(w_atom, whole_atom.at[own_inner], sends, receives, number + 1, peer))
+        weights.append(
+            remote(state_window, states.at[own_inner], sends, receives, number + 2, peer)
+        )
+        returned.append(
+            remote(
+                hidden_rows.at[:, theirs], hidden.at[own_span], sends, receives, number + 3, peer
+            )
+        )
+        number += 4
+    for copy in weights + returned:
+        copy.start()
+    incoming[space] = outgoing[pl.ds(space * blocks, blocks)]
+    whole_atom_in[feat] = w_atom_in[...]
+    whole_atom[own_inner] = w_atom[...]
+    states[own_inner] = state_window[...]
+    hidden[own_span] = hidden_rows[:, pl.ds(pl.multiple_of(feat * width, width), width)]
+    place = lax.broadcasted_iota(jnp.int32, (size, window), 1)
+
+    def spread(block, carry):
+        span = pl.ds(pl.multiple_of(block * size, size), size)
+        pair = ends[span]
+        left_hot[span] = jnp.where(place == pair[:, 0:1], 1.0, 0.0).astype(jnp.bfloat16)
+        right_hot[span] = jnp.where(place == pair[:, 1:2], 1.0, 0.0).astype(jnp.bfloat16)
+        return carry
+
+    lax.fori_loop(0, blocks, spread, 0)
+    for copy in crossing:
+        copy.wait()
+    own_channels = pl.ds(pl.multiple_of(feat * channels, channels), channels)
+    for block in range(blocks):
+        span = slice(block * size, (block + 1) * size)
+        total = incoming[0, block].astype(jnp.float32)
+        for source in range(1, spaces):
+            total = total + incoming[source, block].astype(jnp.float32)
+        lane = lax.broadcasted_iota(jnp.int32, (channels, size), 1)
+        mask = jnp.where(lane < fill[block], 1.0, 0.0)
+        summed[:channels, span] = (total * mask).astype(jnp.bfloat16)
+        summed[channels:, span] = mask.astype(jnp.bfloat16)
+    message[own_channels] = summed[:channels]
+    spreading = []
+    for peer in peers:
+        spreading.append(
+            remote(
+                summed.at[:channels], message.at[own_channels], sends, receives, number, peer
+            )
+        )
+        number += 1
+    partial = jnp.dot(summed[...], right_hot[...], preferred_element_type=jnp.float32)
+    halo_out[0] = partial[:, :atoms]
+    halo_out[1] = partial[:, 2 * atoms :]
+    halos = [
+        remote(halo_out.at[0], halo_in.at[0], sends, receives, number, sides[0]),
+        remote(halo_out.at[1], halo_in.at[1], sends, receives, number + 1, sides[1]),
+    ]
+    number += 2
+    for copy in halos + spreading:
+        copy.start()
+    for copy in halos:
+        copy.wait()
+    full = partial[:, atoms : 2 * atoms] + halo_in[0] + halo_in[1]
+    mean[...] = (full[:channels] / jnp.maximum(full[channels:], 1.0)).astype(jnp.bfloat16)
+    sharing = []
+    for peer in peers:
+        spot = means.at[own_channels, atoms : 2 * atoms]
+        sharing.append(remote(mean, spot, sends, receives, number, peer))
+        number += 1
+    for near in range(feats):
+        for side in range(2):
+            peer = ((lower, upper)[side], lax.rem(feat + near, feats))
+            columns = slice(2 * atoms, 3 * atoms) if side == 0 else slice(0, atoms)
+            spot = means.at[own_channels, columns]
+            sharing.append(remote(mean, spot, sends, receives, number, peer))
+            number += 1
+    for copy in sharing:
+        copy.start()
+    means[own_channels, atoms : 2 * atoms] = mean[...]
+    for copy in sharing + weights:
+        copy.wait()
+    first = (((0,), (0,)), ((), ()))
+    last = (((1,), (1,)), ((), ()))
+    mean_in = jnp.concatenate(
+        [
+            lax.dot_general(
+                whole_atom_in[near], means[...], first, preferred_element_type=jnp.float32
+            ).astype(jnp.bfloat16)
+            for near in range(feats)
+        ],
+        axis=0,
+    )
+    pre = lax.dot_general(whole_atom[...], mean_in, first, preferred_element_type=jnp.float32)
+    window_atoms[...] = (states[...].astype(jnp.float32) + silu(pre)).astype(jnp.bfloat16)
+    atom_out[...] = window_atoms[own_inner, atoms : 2 * atoms]
+    for copy in spreading + returned:
+        copy.wait()
+    row = lax.broadcasted_iota(jnp.int32, (size, width), 0)
+
+    def finish(block, carry):
+        span = pl.ds(pl.multiple_of(block * size, size), size)
+        left = lax.dot_general(
+            left_hot[span], window_atoms[...], last, preferred_element_type=jnp.float32
+        ).astype(jnp.bfloat16)
+        right = lax.dot_general(
+            right_hot[span], window_atoms[...], last, preferred_element_type=jnp.float32
+        ).astype(jnp.bfloat16)
+        mixed = jnp.dot(left, w_left[...], preferred_element_type=jnp.float32) + jnp.dot(
+            right, w_right[...], preferred_element_type=jnp.float32
+        )
+        gate = lax.dot_general(
+            message[:, span], w_gate[...], first, preferred_element_type=jnp.float32
+        )
+        update = (hidden[span].astype(jnp.float32) + silu(mixed)) / (1.0 + jnp.exp(-gate))
+        old = bond[span].astype(jnp.float32)
+        bond_out[span] = (old + jnp.where(row < fill[block], update, 0.0)).astype(jnp.bfloat16)
+        return carry
+
+    lax.fori_loop(0, blocks, finish, 0)
+
+
+def fast(
+    bond_state,
+    block_fill,
+    w_in,
+    w_down,
+    pair_coef,
+    pair_source,
+    pair_owner,
+    pair_target,
+    w_gate,
+    w_atom_in,
+    atom_state,
+    w_atom,
+    bond_ends,
+    w_left,
+    w_right,
+):
+    spaces, feats = lax.axis_size("space"), lax.axis_size("feat")
+    slots, width = bond_state.shape
+    blocks = block_fill.shape[0]
+    size = slots // blocks
+    pairs = pair_source.shape[0]
+    features, units = w_in.shape
+    channels = w_down.shape[1]
+    own_channels = channels // feats
+    share = slots // feats
+    inner, atoms = atom_state.shape
+    half, single = jnp.bfloat16, jnp.float32
+    vmem = pl.BlockSpec(memory_space=pltpu.VMEM)
+    smem = pl.BlockSpec(memory_space=pltpu.SMEM)
+    dma = pltpu.SemaphoreType.DMA
+    first_copies = 4 * (feats - 1) + 2
+    angular, hidden_rows, state_window = pl.pallas_call(
+        functools.partial(bond_kernel, feats),
+        out_shape=(
+            jax.ShapeDtypeStruct((own_channels, slots), half),
+            jax.ShapeDtypeStruct((share, units * feats), half),
+            jax.ShapeDtypeStruct((inner, 3 * atoms), half),
+        ),
+        in_specs=[smem] + [vmem] * 4,
+        out_specs=(vmem, vmem, vmem),
+        scratch_shapes=[
+            pltpu.VMEM((share, features), half),
+            pltpu.VMEM((features, units * feats), half),
+            pltpu.VMEM((features, channels), half),
+            pltpu.VMEM((channels, share), half),
+            dma((first_copies,)),
+            dma((first_copies,)),
+        ],
+        compiler_params=pltpu.CompilerParams(collective_id=0, has_side_effects=True),
+        name="bond_mlp",
+    )(block_fill, bond_state, w_in, w_down, atom_state)
+    steps = 4 if pairs % 4 == 0 else 1
+    part = pairs // steps
+    outgoing = pl.pallas_call(
+        functools.partial(pair_kernel, steps, blocks),
+        grid=(steps,),
+        out_shape=jax.ShapeDtypeStruct((spaces * blocks, own_channels, size), half),
+        in_specs=[
+            smem,
+            smem,
+            smem,
+            pl.BlockSpec((own_channels, slots), lambda i: (0, 0)),
+            pl.BlockSpec((part, size, size), lambda i: (i, 0, 0)),
+        ],
+        out_specs=pl.BlockSpec((spaces * blocks, own_channels, size), lambda i: (0, 0, 0)),
+        scratch_shapes=[pltpu.VMEM((spaces * blocks, own_channels, size), single)],
+        name="pair_sums",
+    )(pair_source, pair_owner.reshape(pairs), pair_target, angular, pair_coef)
+    last_copies = 4 * (feats - 1) + (feats - 1) + 2 + (feats - 1) + 2 * feats
+    bond_out, atom_out = pl.pallas_call(
+        functools.partial(update_kernel, spaces, feats),
+        out_shape=(
+            jax.ShapeDtypeStruct((slots, width), half),
+            jax.ShapeDtypeStruct((inner, atoms), half),
+        ),
+        in_specs=[smem] + [vmem] * 10,
+        out_specs=(vmem, vmem),
+        scratch_shapes=[
+            pltpu.VMEM((spaces, blocks, own_channels, size), half),
+            pltpu.VMEM((slots, 3 * atoms), half),
+            pltpu.VMEM((slots, 3 * atoms), half),
+            pltpu.VMEM((2 * own_channels, slots), half),
+            pltpu.VMEM((channels, slots), half),
+            pltpu.VMEM((2, 2 * own_channels, atoms), single),
+            pltpu.VMEM((2, 2 * own_channels, atoms), single),
+            pltpu.VMEM((own_channels, atoms), half),
+            pltpu.VMEM((channels, 3 * atoms), half),
+            pltpu.VMEM((inner * feats, 3 * atoms), half),
+            pltpu.VMEM((feats,) + w_atom_in.shape, half),
+            pltpu.VMEM((inner * feats, w_atom.shape[1]), half),
+            pltpu.VMEM((slots, width), half),
+            pltpu.VMEM((inner * feats, 3 * atoms), half),
+            dma((spaces,)),
+            dma((spaces,)),
+            dma((last_copies,)),
+            dma((last_copies,)),
+        ],
+        compiler_params=pltpu.CompilerParams(
+            collective_id=1, has_side_effects=True, vmem_limit_bytes=60 * 2**20
+        ),
+        name="bond_update",
+    )(
+        block_fill,
+        outgoing,
+        hidden_rows,
+        state_window,
+        bond_state,
+        bond_ends.T,
+        w_gate,
+        w_atom_in,
+        w_atom,
+        w_left,
+        w_right,
+    )
+    return (bond_out, atom_out)
+
+
 def solution(mesh):
     placed = (
         P("space", "feat"),
@@ -181,8 +652,10 @@
         P(None, "feat"),
         P(None, "feat"),
     )
+    spaces = mesh.shape["space"]
+    body = fast if 4 <= spaces <= 16 else local
     return jax.shard_map(
-        local,
+        body,
         mesh=mesh,
         in_specs=placed,
         out_specs=(P("space", "feat"), P("feat", "space")),

time: 173 us -> 80.3 us (0.46)
  Pallas kernels: 0 us -> 73.1 us
  other arithmetic: 30.3 us -> 0 us
  blocking collectives: 30.3 us -> 0 us
  waiting for transfers between devices: 29.3 us -> 0 us
  starting transfers between devices: 27.6 us -> 0 us
  local copies, waits for them, and re-layouts: 27.5 us -> 6.13 us
  between operations: 14.4 us -> 0.66 us
  matrix products: 13.1 us -> 0 us
    pallas_call x0 -> x3, Pallas kernels: none -> 73.1 us  [the longest x1 42.3 us: fast(): pl.pallas_call(functools.partial(update_kernel, spaces, feats), out_shape...]
    all_gather x4 -> x0, blocking collectives: 30.3 us -> none  [the longest x1 10.8 us: local(): lax.all_gather(w_in, 'feat', axis=1, tiled=True)]
    scatter-add x2 -> x0, other arithmetic: 24.9 us -> none  [the longest x1 13.2 us: local(): jax.ops.segment_sum(real_mask, bond_ends[1], num_segments=window)]
    unnamed x3 -> x0, waiting for transfers between devices: 17.3 us -> none
    gather x3 -> x0, local copies, waits for them, and re-layouts: 15.7 us -> none  [the longest x1 7.5 us: local(): left_rows = jnp.take(neighbours, bond_ends[0], axis=1)]
    ppermute x6 -> x0, starting transfers between devices: 14.3 us -> none  [the longest x4 9.55 us: passed_along(): return lax.ppermute(value, axis, pairs)]
    all_to_all x2 -> x0, starting transfers between devices: 13.2 us -> none  [the longest x1 7.28 us: local(): lax.all_to_all(labels.reshape(spaces, capacity), 'space', split_axis=0, c...]
    dot_general x9 -> x0, matrix products: 13.1 us -> none  [the longest x1 4.09 us: local(): jnp.einsum('cpj,pij->pci', sources, pair_coef, preferred_element_type=jnp...]
  transfers between devices with their start and end apart: 10 -> 0, of which waited for: 6 -> 0; matrix products, arithmetic and copies ran while one was open for 27% -> 0% of each run, Pallas kernels for 0% -> 0%
where the time goes in v1:
time: 80.3 us; the launch traced here: 79.9 us
  Pallas kernels  73.1 us (91%)
  local copies, waits for them, and re-layouts  6.13 us (8%)
    pallas_call x1, Pallas kernels, fast(): pl.pallas_call(functools.partial(update_kernel, spaces, feats), out_shape...  42.3 us
    pallas_call x1, Pallas kernels, fast(): pl.pallas_call(functools.partial(bond_kernel, feats), out_shape=(jax.Shap...  25.2 us
    unnamed x6, local copies, waits for them, and re-layouts  6.13 us
    pallas_call x1, Pallas kernels, fast(): pl.pallas_call(functools.partial(pair_kernel, steps, blocks), grid=(steps...  5.54 us

profile of v1, /device:TPU:0, one launch (start us, length us, event | category | flops | bytes accessed | tf_op | source)
XLA Modules:
  0.0 79.9 jit_solution(7528822429028351914)
XLA Ops:
  0.6 0.0 copy-start
  0.6 1.4 %copy.17.w_down = bf16[128,64]{1,0:T(8,128)(2,1)} copy(bf16[128,64]{0,1:T(8,128)(2,1)} %param.18) | data formatting | bytes 32768 | tf_op args[3]
  2.1 25.2 %bond_mlp.1 = (bf16[16,2048]{1,0:T(8,128)(2,1)}, bf16[512,512]{1,0:T(8,128)(2,1)}, bf16[64,1536]{1,0:T(8,128)(2,1)}) custom-call(s32[16]{0:T(128)} %fill.3, bf16[2048,128]{1,0:T(8,128)(2,1)} %bond.3, bf16[512,128]{1,0:T(8,128)(2,1)} %w_in.1, bf16[128,64]{1,0:T(8,128)(2,1)} %copy.17.w_down, bf16[64,512]{1,0:T(8,128)(2,1)} %state.1), custom_call_target="tpu_custom_call" | custom-call | tf_op jit(solution)/shard_map/bond_mlp/pallas_call | solution.py:551
  27.3 5.5 %pair_sums.1.outgoing = bf16[128,16,128]{2,1,0:T(8,128)(2,1)} custom-call(s32[112]{0:T(128)} %source.1, s32[112]{0:T(128)} %bitcast.3, s32[112]{0:T(128)} %target.1, bf16[16,2048]{1,0:T(8,128)(2,1)} %get-tuple-element.5.angular, bf16[112,128,128]{2,1,0:T(8,128)(2,1)} %coefficients.1), custom_call_target="tpu_custom_call" | custom-call | tf_op jit(solution)/shard_map/pair_sums/pallas_call | solution.py:573
  32.8 0.0 copy-done
  32.8 1.3 %copy.18 = s32[2,2048]{0,1:T(8,128)} copy(s32[2,2048]{1,0:T(2,128)S(1)} %copy-done) | data formatting | bytes 32768 | tf_op args[12]
  34.2 42.3 %bond_update.1 = (bf16[2048,128]{1,0:T(8,128)(2,1)}, bf16[64,512]{1,0:T(8,128)(2,1)}) custom-call(s32[16]{0:T(128)} %fill.3, bf16[128,16,128]{2,1,0:T(8,128)(2,1)} %pair_sums.1.outgoing, bf16[512,512]{1,0:T(8,128)(2,1)} %get-tuple-element.6.hidden_rows, bf16[64,1536]{1,0:T(8,128)(2,1)} %get-tuple-element.7.state_window, bf16[2048,128]{1,0:T(8,128)(2,1)} %bond.3, ...), custom_call_target="tpu_custom_call" | custom-call | tf_op jit(solution)/shard_map/bond_update/pallas_call | solution.py:589
  76.5 1.9 %copy.21 = bf16[2048,128]{1,0:T(8,128)(2,1)} copy(bf16[2048,128]{1,0:T(8,128)(2,1)} %get-tuple-element.10) | data formatting | bytes 1048576
  78.4 1.5 %copy.22 = bf16[64,512]{1,0:T(8,128)(2,1)} copy(bf16[64,512]{1,0:T(8,128)(2,1)} %get-tuple-element.11) | data formatting | bytes 131072
Async XLA Ops:
  0.6 32.2 %copy-start = (s32[2,2048]{1,0:T(2,128)S(1)}, s32[2,2048]{1,0:T(2,128)}, u32[]{:S(2)}) copy-start(s32[2,2048]{1,0:T(2,128)} %param.27) | copy-start | bytes 49156

commit v2 on v1

--- a/solution.py
+++ b/solution.py
@@ -232,13 +232,35 @@
     own_units = pl.ds(pl.multiple_of(feat * units, units), units)
     copies, late = [], []
     number = 0
+    relayed = feats == 4
+    if relayed:
+        partner = (space, feat + 1 - 2 * lax.rem(feat, 2))
+        opposite = (space, lax.rem(feat + 2, 4))
+        across_units = pl.ds(pl.multiple_of(opposite[1] * units, units), units)
+        across = remote(
+            w_in, whole_in.at[:, own_units], sends, receives, 4 * (feats - 1) + 2, opposite
+        )
+        beside = remote(
+            w_in, whole_in.at[:, own_units], sends, receives, 4 * (feats - 1) + 3, partner
+        )
+        again = remote(
+            whole_in.at[:, across_units],
+            whole_in.at[:, across_units],
+            sends,
+            receives,
+            4 * (feats - 1) + 4,
+            partner,
+        )
+        across.start()
+        beside.start()
     for peer in peers:
         their_rows = pl.ds(pl.multiple_of(peer[1] * share, share), share)
-        copies.append(remote(w_in, whole_in.at[:, own_units], sends, receives, number, peer))
+        if not relayed:
+            copies.append(remote(w_in, whole_in.at[:, own_units], sends, receives, number, peer))
         copies.append(
             remote(bond.at[their_rows], rows.at[:, own_width], sends, receives, number + 1, peer)
         )
-        copies.append(remote(w_down, whole_down.at[own_units], sends, receives, number + 2, peer))
+        copies.append(remote(w_down, whole_down.at[:, own_units], sends, receives, number + 2, peer))
         number += 3
     late.append(
         remote(state, state_window.at[:, 2 * atoms :], sends, receives, number, lower)
@@ -252,15 +274,19 @@
     own_rows = pl.ds(pl.multiple_of(feat * share, share), share)
     rows[:, own_width] = bond[own_rows]
     whole_in[:, own_units] = w_in[...]
-    whole_down[own_units] = w_down[...]
+    whole_down[:, own_units] = w_down[...]
     state_window[:, atoms : 2 * atoms] = state[...]
+    if relayed:
+        across.wait()
+        again.start()
+        copies = [beside, again] + copies
     for copy in copies:
         copy.wait()
     hidden[...] = silu(
         jnp.dot(rows[...], whole_in[...], preferred_element_type=jnp.float32)
     ).astype(jnp.bfloat16)
     sums = lax.dot_general(
-        whole_down[...], hidden[...], (((0,), (1,)), ((), ())), preferred_element_type=jnp.float32
+        whole_down[...], hidden[...], (((1,), (1,)), ((), ())), preferred_element_type=jnp.float32
     )
     for part in range(share // block_size):
         limit = fill[feat * (share // block_size) + part]
@@ -352,6 +378,7 @@
     whole_atom,
     hidden,
     window_atoms,
+    table,
     space_sends,
     space_receives,
     sends,
@@ -414,13 +441,14 @@
     whole_atom[own_inner] = w_atom[...]
     states[own_inner] = state_window[...]
     hidden[own_span] = hidden_rows[:, pl.ds(pl.multiple_of(feat * width, width), width)]
-    place = lax.broadcasted_iota(jnp.int32, (size, window), 1)
+    place = lax.broadcasted_iota(jnp.int16, (size, window), 1)
+    one, zero = jnp.bfloat16(1), jnp.bfloat16(0)
 
     def spread(block, carry):
         span = pl.ds(pl.multiple_of(block * size, size), size)
-        pair = ends[span]
-        left_hot[span] = jnp.where(place == pair[:, 0:1], 1.0, 0.0).astype(jnp.bfloat16)
-        right_hot[span] = jnp.where(place == pair[:, 1:2], 1.0, 0.0).astype(jnp.bfloat16)
+        pair = ends[span].astype(jnp.int16)
+        left_hot[span] = jnp.where(place == pair[:, 0:1], one, zero)
+        right_hot[span] = jnp.where(place == pair[:, 1:2], one, zero)
         return carry
 
     lax.fori_loop(0, blocks, spread, 0)
@@ -453,7 +481,7 @@
         remote(halo_out.at[1], halo_in.at[1], sends, receives, number + 1, sides[1]),
     ]
     number += 2
-    for copy in halos + spreading:
+    for copy in halos:
         copy.start()
     for copy in halos:
         copy.wait()
@@ -471,13 +499,12 @@
             spot = means.at[own_channels, columns]
             sharing.append(remote(mean, spot, sends, receives, number, peer))
             number += 1
-    for copy in sharing:
+    for copy in sharing + spreading:
         copy.start()
     means[own_channels, atoms : 2 * atoms] = mean[...]
     for copy in sharing + weights:
         copy.wait()
     first = (((0,), (0,)), ((), ()))
-    last = (((1,), (1,)), ((), ()))
     mean_in = jnp.concatenate(
         [
             lax.dot_general(
@@ -492,15 +519,18 @@
     atom_out[...] = window_atoms[own_inner, atoms : 2 * atoms]
     for copy in spreading + returned:
         copy.wait()
+    table[...] = window_atoms[...].T
     row = lax.broadcasted_iota(jnp.int32, (size, width), 0)
-
-    def finish(block, carry):
-        span = pl.ds(pl.multiple_of(block * size, size), size)
-        left = lax.dot_general(
-            left_hot[span], window_atoms[...], last, preferred_element_type=jnp.float32
+    grouped = 4 if blocks % 4 == 0 else 1
+    piece = grouped * size
+
+    def finish(turn, carry):
+        span = pl.ds(pl.multiple_of(turn * piece, piece), piece)
+        left = jnp.dot(
+            left_hot[span], table[...], preferred_element_type=jnp.float32
         ).astype(jnp.bfloat16)
-        right = lax.dot_general(
-            right_hot[span], window_atoms[...], last, preferred_element_type=jnp.float32
+        right = jnp.dot(
+            right_hot[span], table[...], preferred_element_type=jnp.float32
         ).astype(jnp.bfloat16)
         mixed = jnp.dot(left, w_left[...], preferred_element_type=jnp.float32) + jnp.dot(
             right, w_right[...], preferred_element_type=jnp.float32
@@ -510,10 +540,14 @@
         )
         update = (hidden[span].astype(jnp.float32) + silu(mixed)) / (1.0 + jnp.exp(-gate))
         old = bond[span].astype(jnp.float32)
-        bond_out[span] = (old + jnp.where(row < fill[block], update, 0.0)).astype(jnp.bfloat16)
+        kept = [
+            jnp.where(row < fill[turn * grouped + i], update[i * size : (i + 1) * size], 0.0)
+            for i in range(grouped)
+        ]
+        bond_out[span] = (old + jnp.concatenate(kept, axis=0)).astype(jnp.bfloat16)
         return carry
 
-    lax.fori_loop(0, blocks, finish, 0)
+    lax.fori_loop(0, blocks // grouped, finish, 0)
 
 
 def fast(
@@ -547,7 +581,7 @@
     vmem = pl.BlockSpec(memory_space=pltpu.VMEM)
     smem = pl.BlockSpec(memory_space=pltpu.SMEM)
     dma = pltpu.SemaphoreType.DMA
-    first_copies = 4 * (feats - 1) + 2
+    first_copies = 4 * (feats - 1) + 5
     angular, hidden_rows, state_window = pl.pallas_call(
         functools.partial(bond_kernel, feats),
         out_shape=(
@@ -560,14 +594,14 @@
         scratch_shapes=[
             pltpu.VMEM((share, features), half),
             pltpu.VMEM((features, units * feats), half),
-            pltpu.VMEM((features, channels), half),
+            pltpu.VMEM((channels, features), half),
             pltpu.VMEM((channels, share), half),
             dma((first_copies,)),
             dma((first_copies,)),
         ],
         compiler_params=pltpu.CompilerParams(collective_id=0, has_side_effects=True),
         name="bond_mlp",
-    )(block_fill, bond_state, w_in, w_down, atom_state)
+    )(block_fill, bond_state, w_in, w_down.T, atom_state)
     steps = 4 if pairs % 4 == 0 else 1
     part = pairs // steps
     outgoing = pl.pallas_call(
@@ -609,6 +643,7 @@
             pltpu.VMEM((inner * feats, w_atom.shape[1]), half),
             pltpu.VMEM((slots, width), half),
             pltpu.VMEM((inner * feats, 3 * atoms), half),
+            pltpu.VMEM((3 * atoms, inner * feats), half),
             dma((spaces,)),
             dma((spaces,)),
             dma((last_copies,)),

time: 80.3 us -> 67.8 us (0.84)
  Pallas kernels: 73.1 us -> 62.1 us
  local copies, waits for them, and re-layouts: 6.13 us -> 4.69 us
    pallas_call x1, Pallas kernels: 42.3 us -> 34.8 us  [fast(): pl.pallas_call(functools.partial(update_kernel, spaces, feats), out_shape...]
    pallas_call x1, Pallas kernels: 25.2 us -> 21.8 us  [fast(): pl.pallas_call(functools.partial(bond_kernel, feats), out_shape=(jax.Shap...]
    unnamed x6 -> x5, local copies, waits for them, and re-layouts: 6.13 us -> 4.69 us
where the time goes in v2:
time: 67.8 us; the launch traced here: 67.5 us
  Pallas kernels  62.1 us (92%)
  local copies, waits for them, and re-layouts  4.69 us (7%)
    pallas_call x1, Pallas kernels, fast(): pl.pallas_call(functools.partial(update_kernel, spaces, feats), out_shape...  34.8 us
    pallas_call x1, Pallas kernels, fast(): pl.pallas_call(functools.partial(bond_kernel, feats), out_shape=(jax.Shap...  21.8 us
    pallas_call x1, Pallas kernels, fast(): pl.pallas_call(functools.partial(pair_kernel, steps, blocks), grid=(steps...  5.54 us
    unnamed x5, local copies, waits for them, and re-layouts  4.69 us

profile of v2, /device:TPU:0, one launch (start us, length us, event | category | flops | bytes accessed | tf_op | source)
XLA Modules:
  0.0 67.5 jit_solution(12573840107123022717)
XLA Ops:
  0.6 0.0 copy-start
  0.6 21.8 %bond_mlp.1 = (bf16[16,2048]{1,0:T(8,128)(2,1)}, bf16[512,512]{1,0:T(8,128)(2,1)}, bf16[64,1536]{1,0:T(8,128)(2,1)}) custom-call(s32[16]{0:T(128)} %fill.3, bf16[2048,128]{1,0:T(8,128)(2,1)} %bond.3, bf16[512,128]{1,0:T(8,128)(2,1)} %w_in.1, bf16[64,128]{1,0:T(8,128)(2,1)} %bitcast.4, bf16[64,512]{1,0:T(8,128)(2,1)} %state.1), custom_call_target="tpu_custom_call" | custom-call | tf_op jit(solution)/shard_map/bond_mlp/pallas_call | solution.py:585
  22.4 5.5 %pair_sums.1.outgoing = bf16[128,16,128]{2,1,0:T(8,128)(2,1)} custom-call(s32[112]{0:T(128)} %source.1, s32[112]{0:T(128)} %bitcast.5, s32[112]{0:T(128)} %target.1, bf16[16,2048]{1,0:T(8,128)(2,1)} %get-tuple-element.5.angular, bf16[112,128,128]{2,1,0:T(8,128)(2,1)} %coefficients.1), custom_call_target="tpu_custom_call" | custom-call | tf_op jit(solution)/shard_map/pair_sums/pallas_call | solution.py:607
  28.0 0.0 copy-done
  28.0 1.3 %copy.17 = s32[2,2048]{0,1:T(8,128)} copy(s32[2,2048]{1,0:T(2,128)S(1)} %copy-done) | data formatting | bytes 32768 | tf_op args[12]
  29.3 34.8 %bond_update.1 = (bf16[2048,128]{1,0:T(8,128)(2,1)}, bf16[64,512]{1,0:T(8,128)(2,1)}) custom-call(s32[16]{0:T(128)} %fill.3, bf16[128,16,128]{2,1,0:T(8,128)(2,1)} %pair_sums.1.outgoing, bf16[512,512]{1,0:T(8,128)(2,1)} %get-tuple-element.6.hidden_rows, bf16[64,1536]{1,0:T(8,128)(2,1)} %get-tuple-element.7.state_window, bf16[2048,128]{1,0:T(8,128)(2,1)} %bond.3, ...), custom_call_target="tpu_custom_call" | custom-call | tf_op jit(solution)/shard_map/bond_update/pallas_call | solution.py:623
  64.1 1.9 %copy.20 = bf16[2048,128]{1,0:T(8,128)(2,1)} copy(bf16[2048,128]{1,0:T(8,128)(2,1)} %get-tuple-element.10) | data formatting | bytes 1048576
  66.0 1.5 %copy.21 = bf16[64,512]{1,0:T(8,128)(2,1)} copy(bf16[64,512]{1,0:T(8,128)(2,1)} %get-tuple-element.11) | data formatting | bytes 131072
Async XLA Ops:
  0.6 27.3 %copy-start = (s32[2,2048]{1,0:T(2,128)S(1)}, s32[2,2048]{1,0:T(2,128)}, u32[]{:S(2)}) copy-start(s32[2,2048]{1,0:T(2,128)} %param.27) | copy-start | bytes 49156

commit v3 on v2

--- a/solution.py
+++ b/solution.py
@@ -364,6 +364,8 @@
     w_right,
     bond_out,
     atom_out,
+    first_in,
+    middle,
     incoming,
     left_hot,
     right_hot,
@@ -398,23 +400,24 @@
     lower, upper = down(space, -1), down(space, 1)
     sides = [(lower, feat), (upper, feat)]
     diagonal = [(side, peer[1]) for side in (lower, upper) for peer in peers]
-    far = [(down(space, step), feat) for step in range(2, spaces - 1)]
+    half_count = spaces // 2
+    parity = lax.rem(space, 2)
+    partner = (space + 1 - 2 * parity, feat)
+    order = sorted(range(1, half_count), key=lambda k: -min(k, half_count - k)) + [0]
+    far = [(down(space, 2 * step), feat) for step in range(1, half_count)]
     greet(peers + sides + diagonal + far)
-    crossing = []
-    for step in range(1, spaces):
-        goal = down(space, step)
-        crossing.append(
-            remote(
-                outgoing.at[pl.ds(goal * blocks, blocks)],
-                incoming.at[space],
-                space_sends,
-                space_receives,
-                step,
-                (goal, feat),
-            )
-        )
-    for copy in crossing:
-        copy.start()
+    paired, crossing = {}, []
+    for step in order:
+        goal = down(space, 2 * step) + 1 - 2 * parity
+        paired[step] = remote(
+            outgoing.at[pl.ds(goal * blocks, blocks)],
+            first_in.at[step],
+            space_sends,
+            space_receives,
+            step,
+            partner,
+        )
+        paired[step].start()
     own_inner = pl.ds(pl.multiple_of(feat * inner, inner), inner)
     own_span = pl.ds(pl.multiple_of(feat * share, share), share)
     weights, returned = [], []
@@ -436,7 +439,26 @@
         number += 4
     for copy in weights + returned:
         copy.start()
-    incoming[space] = outgoing[pl.ds(space * blocks, blocks)]
+    for step in order:
+        goal = down(space, 2 * step)
+        paired[step].wait()
+        both = outgoing[pl.ds(goal * blocks, blocks)].astype(jnp.float32) + first_in[
+            step
+        ].astype(jnp.float32)
+        place_of = incoming if step == 0 else middle
+        place_of[step] = both.astype(jnp.bfloat16)
+        if step:
+            crossing.append(
+                remote(
+                    middle.at[step],
+                    incoming.at[step],
+                    space_sends,
+                    space_receives,
+                    half_count + step,
+                    (goal, feat),
+                )
+            )
+            crossing[-1].start()
     whole_atom_in[feat] = w_atom_in[...]
     whole_atom[own_inner] = w_atom[...]
     states[own_inner] = state_window[...]
@@ -446,7 +468,7 @@
 
     def spread(block, carry):
         span = pl.ds(pl.multiple_of(block * size, size), size)
-        pair = ends[span].astype(jnp.int16)
+        pair = ends[:, span].T.astype(jnp.int16)
         left_hot[span] = jnp.where(place == pair[:, 0:1], one, zero)
         right_hot[span] = jnp.where(place == pair[:, 1:2], one, zero)
         return carry
@@ -458,7 +480,7 @@
     for block in range(blocks):
         span = slice(block * size, (block + 1) * size)
         total = incoming[0, block].astype(jnp.float32)
-        for source in range(1, spaces):
+        for source in range(1, half_count):
             total = total + incoming[source, block].astype(jnp.float32)
         lane = lax.broadcasted_iota(jnp.int32, (channels, size), 1)
         mask = jnp.where(lane < fill[block], 1.0, 0.0)
@@ -629,7 +651,9 @@
         in_specs=[smem] + [vmem] * 10,
         out_specs=(vmem, vmem),
         scratch_shapes=[
-            pltpu.VMEM((spaces, blocks, own_channels, size), half),
+            pltpu.VMEM((spaces // 2, blocks, own_channels, size), half),
+            pltpu.VMEM((spaces // 2, blocks, own_channels, size), half),
+            pltpu.VMEM((spaces // 2, blocks, own_channels, size), half),
             pltpu.VMEM((slots, 3 * atoms), half),
             pltpu.VMEM((slots, 3 * atoms), half),
             pltpu.VMEM((2 * own_channels, slots), half),
@@ -659,7 +683,7 @@
         hidden_rows,
         state_window,
         bond_state,
-        bond_ends.T,
+        bond_ends,
         w_gate,
         w_atom_in,
         w_atom,
@@ -688,7 +712,7 @@
         P(None, "feat"),
     )
     spaces = mesh.shape["space"]
-    body = fast if 4 <= spaces <= 16 else local
+    body = fast if spaces in range(4, 17, 2) else local
     return jax.shard_map(
         body,
         mesh=mesh,

time: 67.8 us -> 66.2 us (0.976)
  local copies, waits for them, and re-layouts: 4.69 us -> 3.34 us
    unnamed x5 -> x2, local copies, waits for them, and re-layouts: 4.69 us -> 3.34 us
where the time goes in v3:
time: 66.2 us; the launch traced here: 65.9 us
  Pallas kernels  61.9 us (94%)
  local copies, waits for them, and re-layouts  3.34 us (5%)
    pallas_call x1, Pallas kernels, fast(): pl.pallas_call(functools.partial(update_kernel, spaces, feats), out_shape...  34.6 us
    pallas_call x1, Pallas kernels, fast(): pl.pallas_call(functools.partial(bond_kernel, feats), out_shape=(jax.Shap...  21.8 us
    pallas_call x1, Pallas kernels, fast(): pl.pallas_call(functools.partial(pair_kernel, steps, blocks), grid=(steps...  5.54 us
    unnamed x2, local copies, waits for them, and re-layouts  3.34 us

profile of v3, /device:TPU:0, one launch (start us, length us, event | category | flops | bytes accessed | tf_op | source)
XLA Modules:
  0.0 65.9 jit_solution(1691098145305453536)
XLA Ops:
  0.6 21.8 %bond_mlp.1 = (bf16[16,2048]{1,0:T(8,128)(2,1)}, bf16[512,512]{1,0:T(8,128)(2,1)}, bf16[64,1536]{1,0:T(8,128)(2,1)}) custom-call(s32[16]{0:T(128)} %fill.3, bf16[2048,128]{1,0:T(8,128)(2,1)} %bond.3, bf16[512,128]{1,0:T(8,128)(2,1)} %w_in.1, bf16[64,128]{1,0:T(8,128)(2,1)} %bitcast.2, bf16[64,512]{1,0:T(8,128)(2,1)} %state.1), custom_call_target="tpu_custom_call" | custom-call | tf_op jit(solution)/shard_map/bond_mlp/pallas_call | solution.py:607
  22.4 5.5 %pair_sums.1.outgoing = bf16[128,16,128]{2,1,0:T(8,128)(2,1)} custom-call(s32[112]{0:T(128)} %source.1, s32[112]{0:T(128)} %bitcast.3, s32[112]{0:T(128)} %target.1, bf16[16,2048]{1,0:T(8,128)(2,1)} %get-tuple-element.5.angular, bf16[112,128,128]{2,1,0:T(8,128)(2,1)} %coefficients.1), custom_call_target="tpu_custom_call" | custom-call | tf_op jit(solution)/shard_map/pair_sums/pallas_call | solution.py:629
  28.0 34.6 %bond_update.1 = (bf16[2048,128]{1,0:T(8,128)(2,1)}, bf16[64,512]{1,0:T(8,128)(2,1)}) custom-call(s32[16]{0:T(128)} %fill.3, bf16[128,16,128]{2,1,0:T(8,128)(2,1)} %pair_sums.1.outgoing, bf16[512,512]{1,0:T(8,128)(2,1)} %get-tuple-element.6.hidden_rows, bf16[64,1536]{1,0:T(8,128)(2,1)} %get-tuple-element.7.state_window, bf16[2048,128]{1,0:T(8,128)(2,1)} %bond.3, ...), custom_call_target="tpu_custom_call" | custom-call | tf_op jit(solution)/shard_map/bond_update/pallas_call | solution.py:645
  62.5 1.9 %copy.19 = bf16[2048,128]{1,0:T(8,128)(2,1)} copy(bf16[2048,128]{1,0:T(8,128)(2,1)} %get-tuple-element.10) | data formatting | bytes 1048576
  64.4 1.5 %copy.20 = bf16[64,512]{1,0:T(8,128)(2,1)} copy(bf16[64,512]{1,0:T(8,128)(2,1)} %get-tuple-element.11) | data formatting | bytes 131072

commit v4 on v3

--- a/solution.py
+++ b/solution.py
@@ -316,7 +316,7 @@
     step = pl.program_id(0)
     count = coefficients.shape[0]
     block_size = coefficients.shape[1]
-    group = 14 if count % 14 == 0 else 1
+    group = 28 if count % 28 == 0 else 1
 
     @pl.when(step == 0)
     def clear():

time: 66.2 us -> 65.8 us (level)
  no operation moved by 1% of the time
where the time goes in v4:
time: 65.8 us; the launch traced here: 65.5 us
  Pallas kernels  61.5 us (93%)
  local copies, waits for them, and re-layouts  3.34 us (5%)
    pallas_call x1, Pallas kernels, fast(): pl.pallas_call(functools.partial(update_kernel, spaces, feats), out_shape...  34.6 us
    pallas_call x1, Pallas kernels, fast(): pl.pallas_call(functools.partial(bond_kernel, feats), out_shape=(jax.Shap...  21.8 us
    pallas_call x1, Pallas kernels, fast(): pl.pallas_call(functools.partial(pair_kernel, steps, blocks), grid=(steps...  5.18 us
    unnamed x2, local copies, waits for them, and re-layouts  3.34 us

profile of v4, /device:TPU:0, one launch (start us, length us, event | category | flops | bytes accessed | tf_op | source)
XLA Modules:
  0.0 65.5 jit_solution(4056589697616477749)
XLA Ops:
  0.6 21.8 %bond_mlp.1 = (bf16[16,2048]{1,0:T(8,128)(2,1)}, bf16[512,512]{1,0:T(8,128)(2,1)}, bf16[64,1536]{1,0:T(8,128)(2,1)}) custom-call(s32[16]{0:T(128)} %fill.3, bf16[2048,128]{1,0:T(8,128)(2,1)} %bond.3, bf16[512,128]{1,0:T(8,128)(2,1)} %w_in.1, bf16[64,128]{1,0:T(8,128)(2,1)} %bitcast.2, bf16[64,512]{1,0:T(8,128)(2,1)} %state.1), custom_call_target="tpu_custom_call" | custom-call | tf_op jit(solution)/shard_map/bond_mlp/pallas_call | solution.py:607
  22.4 5.2 %pair_sums.1.outgoing = bf16[128,16,128]{2,1,0:T(8,128)(2,1)} custom-call(s32[112]{0:T(128)} %source.1, s32[112]{0:T(128)} %bitcast.3, s32[112]{0:T(128)} %target.1, bf16[16,2048]{1,0:T(8,128)(2,1)} %get-tuple-element.5.angular, bf16[112,128,128]{2,1,0:T(8,128)(2,1)} %coefficients.1), custom_call_target="tpu_custom_call" | custom-call | tf_op jit(solution)/shard_map/pair_sums/pallas_call | solution.py:629
  27.6 34.6 %bond_update.1 = (bf16[2048,128]{1,0:T(8,128)(2,1)}, bf16[64,512]{1,0:T(8,128)(2,1)}) custom-call(s32[16]{0:T(128)} %fill.3, bf16[128,16,128]{2,1,0:T(8,128)(2,1)} %pair_sums.1.outgoing, bf16[512,512]{1,0:T(8,128)(2,1)} %get-tuple-element.6.hidden_rows, bf16[64,1536]{1,0:T(8,128)(2,1)} %get-tuple-element.7.state_window, bf16[2048,128]{1,0:T(8,128)(2,1)} %bond.3, ...), custom_call_target="tpu_custom_call" | custom-call | tf_op jit(solution)/shard_map/bond_update/pallas_call | solution.py:645
  62.2 1.9 %copy.19 = bf16[2048,128]{1,0:T(8,128)(2,1)} copy(bf16[2048,128]{1,0:T(8,128)(2,1)} %get-tuple-element.10) | data formatting | bytes 1048576
  64.0 1.5 %copy.20 = bf16[64,512]{1,0:T(8,128)(2,1)} copy(bf16[64,512]{1,0:T(8,128)(2,1)} %get-tuple-element.11) | data formatting | bytes 131072
